TPU v7x, 256 devices: a whole 4x4x8 slice. The times are simulated.
256 devices in a mesh: dom: 32 (over y_lo, z, core), repl: 8 (over y_hi, x).
Axes of the slice: x: 4, y: 4 (y_hi: 2, y_lo: 2; y = y_hi * 2 + y_lo), z: 8, core: 2. Of those that a mesh axis runs over, the one named last changes fastest.
Arguments:
- features: float32 [131072, 256], P(('dom', 'repl')), may hold values from -6 to 6
- weight: bfloat16 [256, 256], replicated, may hold values from -0.375 to 0.375
- bias_vector: float32 [256], replicated, may hold values from -0.5 to 0.5
- cotangent: bfloat16 [131072, 256], P(('dom', 'repl')), may hold values from -6 to 6
- near_tiles: bfloat16 [4096, 128, 128], P(('dom', 'repl')), may hold values from -0.1875 to 0.1875
- near_offsets: int32 [256, 33], P(('dom', 'repl')), may hold values from 0 to 16, as said below
- near_cols: int32 [256, 16], P(('dom', 'repl')), may hold values from 0 to 3, as said below
- far_tiles: bfloat16 [256, 32, 1, 128, 128], P(('dom', 'repl')), may hold values from -0.1875 to 0.1875
- far_rows: int32 [256, 32, 1], P(('dom', 'repl')), may hold values from -1 to 31, as said below
- far_cols: int32 [256, 32, 1], P(('dom', 'repl')), may hold values from 0 to 3
Outputs:
- hidden: bfloat16 [131072, 256], P(('dom', 'repl'))
- grad_features: float32 [131072, 256], P(('dom', 'repl'))
- weight_grad: float32 [256, 256], replicated
Inputs may be any that keep to these rules, and one draw needn't show every extreme that they name: `near_offsets`: each row is non-decreasing, begins with 0 and ends with 16. `near_cols`: within one tile row of one device the near tiles' columns differ and rise. `far_rows`: -1 marks an empty slot. A device's slots for the groups whose index of dom lies at most 2 steps from its own around the cycle are never empty.
All inputs are finite; a program needn't handle non-finite values.
Results may differ from a plain program's by a relative error of at most 0.0075.
Values may be sent and summed in bfloat16 or wider, within the bound.
No kernel may reach another device: no remote copies, remote signals or barrier semaphores. Data moves between devices by JAX's collectives and lax.ppermute only.
A program may use at most 128 MiB of HBM per device.

v0:
```python
import math
import jax
import jax.numpy as jnp
from jax import lax
from jax.sharding import PartitionSpec as P


def membership_flags(index, extent, dtype):
    return (index[..., None] == jnp.arange(extent, dtype=jnp.int32)).astype(dtype)


def slot_rows(offsets, slot_count):
    slots = jnp.arange(slot_count, dtype=jnp.int32)
    return jnp.sum((offsets[1:, None] <= slots[None, :]).astype(jnp.int32), axis=0)


def precise_total_sum(form, hot, values):
    return jnp.einsum(form, hot, values, precision=lax.Precision.HIGHEST)


def select(form, hot, values):
    return jnp.einsum(form, hot, values, preferred_element_type=jnp.float32).astype(jnp.bfloat16)


def tile_product(form, tiles, values):
    return jnp.einsum(form, tiles, values, preferred_element_type=jnp.float32)


def activation_grad(pre_values, upstream):
    sigma = jax.nn.sigmoid(pre_values)
    return (upstream.astype(jnp.float32) * sigma * (1.0 + pre_values * (1.0 - sigma))).astype(
        jnp.bfloat16
    )


def on_device(
    features,
    weight,
    bias_vector,
    cotangent,
    near_tiles,
    near_offsets,
    near_cols,
    far_tiles,
    far_rows,
    far_cols,
):
    rows_dev, feat_width = features.shape
    tile_size = near_tiles.shape[1]
    blocks_per_processor = rows_dev // tile_size
    dom_count = lax.axis_size("dom")
    repl_count = lax.axis_size("repl")
    blocks_dom = blocks_per_processor * repl_count
    near_count = near_tiles.shape[0]
    far_block = far_tiles[0]
    far_row_ids = far_rows[0]
    far_col_ids = far_cols[0]
    near_row_ids = slot_rows(near_offsets[0], near_count)
    nearby_column_index = near_cols[0]
    reduced = features.astype(jnp.bfloat16)
    local_block_list = reduced.reshape(blocks_per_processor, tile_size, feat_width)
    nearby_input_rows = select(
        "el,lxh->exh",
        membership_flags(nearby_column_index, blocks_per_processor, jnp.bfloat16),
        local_block_list,
    )
    near_prod = tile_product("qab,qbf->qaf", near_tiles, nearby_input_rows)
    partial_sum = precise_total_sum(
        "qr,qaf->raf", membership_flags(near_row_ids, blocks_dom, jnp.float32), near_prod
    )
    shard_rows = lax.all_gather(reduced, "dom", axis=0, tiled=True)
    range_count = shard_rows.shape[0] // rows_dev
    tiles = far_block
    row_ids = far_row_ids
    col_ids = far_col_ids
    source = shard_rows.reshape(range_count, blocks_per_processor, tile_size, feat_width)
    inputs = select(
        "kqc,kcbf->kqbf", membership_flags(col_ids, blocks_per_processor, jnp.bfloat16), source
    )
    far_prod = tile_product("kqab,kqbf->kqaf", tiles, inputs)
    partial_sum = partial_sum + precise_total_sum(
        "kqr,kqaf->raf", membership_flags(row_ids, blocks_dom, jnp.float32), far_prod
    )
    group_partial = partial_sum.reshape(blocks_dom * tile_size, feat_width)
    summed = lax.psum_scatter(group_partial, "repl", scatter_dimension=0, tiled=True).astype(
        jnp.bfloat16
    )
    pre_act = jnp.dot(summed, weight, preferred_element_type=jnp.float32) + bias_vector
    hidden = jax.nn.silu(pre_act).astype(jnp.bfloat16)
    grad_pre = activation_grad(pre_act, cotangent)
    weight_term = lax.dot_general(
        summed, grad_pre, (((0,), (0,)), ((), ())), preferred_element_type=jnp.float32
    )
    grad_rows = lax.dot_general(
        grad_pre, weight, (((1,), (1,)), ((), ())), preferred_element_type=jnp.float32
    ).astype(jnp.bfloat16)
    group_grad = lax.all_gather(grad_rows, "repl", axis=0, tiled=True)
    node_total = rows_dev * dom_count * repl_count
    weight_grad = lax.psum(weight_term, ("dom", "repl")) * (1.0 / math.sqrt(node_total))
    cluster_block_list = group_grad.reshape(blocks_dom, tile_size, feat_width)
    near_grads = select(
        "om,mgh->ogh", membership_flags(near_row_ids, blocks_dom, jnp.bfloat16), cluster_block_list
    )
    nearby_backward_pass = tile_product("ltp,ltk->lpk", near_tiles, near_grads)
    local_contribution = precise_total_sum(
        "ml,mrx->lrx",
        membership_flags(nearby_column_index, blocks_per_processor, jnp.float32),
        nearby_backward_pass,
    )
    row_count = rows_dev * lax.axis_size("dom")
    tiles = far_block
    row_ids = far_row_ids
    col_ids = far_col_ids
    far_grads = select(
        "kqr,rbf->kqbf", membership_flags(row_ids, blocks_dom, jnp.bfloat16), cluster_block_list
    )
    terms = tile_product("kqab,kqaf->kqbf", tiles, far_grads)
    placed = precise_total_sum(
        "kqc,kqbf->kcbf", membership_flags(col_ids, blocks_per_processor, jnp.float32), terms
    )
    far_grad = lax.psum_scatter(
        placed.reshape(row_count, feat_width).astype(jnp.bfloat16),
        "dom",
        scatter_dimension=0,
        tiled=True,
    ).astype(jnp.float32)
    grad_features = far_grad + local_contribution.reshape(rows_dev, feat_width)
    return (hidden, grad_features, weight_grad)


def solution(mesh):
    placed = (
        P(("dom", "repl"), None),
        P(),
        P(),
        P(("dom", "repl"), None),
        P(("dom", "repl"), None, None),
        P(("dom", "repl"), None),
        P(("dom", "repl"), None),
        P(("dom", "repl"), None, None, None, None),
        P(("dom", "repl"), None, None),
        P(("dom", "repl"), None, None),
    )
    return jax.shard_map(
        on_device,
        mesh=mesh,
        in_specs=placed,
        out_specs=(P(("dom", "repl"), None), P(("dom", "repl"), None), P()),
        check_vma=False,
    )
```

profile of v0, /device:TPU:2, one launch (start us, length us, event | category | flops | bytes accessed | tf_op | source)
XLA Modules:
  0.0 674.9 jit_solution(15560080894403100846)
XLA Ops:
  7.2 1.9 convert_element_type.53
  9.2 1.5 convolution_convert_fusion.1
  10.7 1.9 convolution_bitcast_fusion.3
  12.6 2.3 copy.19
  15.0 0.1 convert_reduce_fusion
  15.2 3.6 fusion.28
  18.7 66.3 %all-gather.3.cloned.1.call-done = bf16[16384,256]{1,0:T(8,128)(2,1)} async-done(((bf16[512,256]{1,0:T(8,128)(2,1)}), bf16[16384,256]{1,0:T(8,128)(2,1)}) %all-gather.3.cloned.1.call-update) | async-done | bytes 8388624 | tf_op jit(solution)/shard_map/all_gather | solution.py:71
  85.0 11.8 %fusion = bf16[32,1,128,256]{3,1,2,0:T(2,128)(2,1)} fusion(bf16[32,4,128,256]{3,2,1,0:T(8,128)(2,1)} %bitcast.65, pred[32,4,1,1]{1,0,2,3:T(32,128)(4,1)S(1)} %get-tuple-element.6), kind=kOutput, calls=%fused_computation.1 | convolution fusion | flops 8388608 | bytes 10485888 | tf_op jit(solution)/shard_map/kqc,kcbf->kqbf/dot_general | solution.py:22
  96.8 8.6 %copy.31 = bf16[32,1,128,256]{2,3,0,1:T(8,128)(2,1)S(1)} copy(bf16[32,1,128,256]{3,1,2,0:T(2,128)(2,1)} %fusion) | data formatting | bytes 4194304 | tf_op jit(solution)/shard_map/kqc,kcbf->kqbf/dot_general | solution.py:22
  105.4 2.7 convolution_bitcast_fusion.1
  108.1 5.5 copy.20
  113.6 5.7 convolution_add_fusion
  119.3 4.4 copy.21
  123.8 89.6 %reduce-scatter.3.cloned.1.call-done = f32[512,256]{1,0:T(8,128)} async-done(((f32[4096,256]{1,0:T(8,128)}), f32[512,256]{1,0:T(8,128)}) %reduce-scatter.3.cloned.1.call-update) | async-done | bytes 524304 | tf_op jit(solution)/shard_map/reduce_scatter | solution.py:85
  213.4 2.2 multiply_convert_fusion.1
  215.7 1.0 convolution_convert_fusion.2
  216.7 0.2 all-reduce.2.cloned.1.call-start
  216.9 1.0 fusion.14
  218.0 57.9 %all-gather.5.cloned.1.call-done = bf16[4096,256]{1,0:T(8,128)(2,1)} async-done(((bf16[512,256]{1,0:T(8,128)(2,1)}), bf16[4096,256]{1,0:T(8,128)(2,1)}) %all-gather.5.cloned.1.call-update) | async-done | bytes 2097168 | tf_op jit(solution)/shard_map/all_gather | solution.py:97
  275.8 2.9 convolution_convert_fusion
  278.8 3.7 convolution_bitcast_fusion
  282.5 5.6 copy.24
  288.1 8.7 %multiply_convert_fusion = bf16[32,4,128,256]{3,2,1,0:T(8,128)(2,1)} fusion(f32[32,128,256]{2,1,0:T(8,128)} %copy.24, f32[32,4]{1,0:T(8,128)S(1)} %get-tuple-element.5), kind=kLoop, calls=%fused_computation | loop fusion | flops 8388608 | bytes 12583424 | tf_op jit(solution)/shard_map/convert_element_type | solution.py:122
  296.8 238.4 %all-reduce.2.cloned.1.call-done = f32[256,256]{1,0:T(8,128)} async-done(((f32[256,256]{1,0:T(8,128)}), f32[256,256]{1,0:T(8,128)}) %all-reduce.2.cloned.1.call-update) | async-done | bytes 262160 | tf_op jit(solution)/shard_map/psum | solution.py:99
  535.2 1.7 broadcast_multiply_fusion
  537.0 1.2 fusion.6
  538.2 0.5 convolution_bitcast_fusion.2
  538.7 2.0 copy.27
  540.8 2.4 fusion.33
  543.2 0.1 copy.28
  543.3 123.3 %reduce-scatter.5.cloned.1.call-done = bf16[512,256]{1,0:T(8,128)(2,1)} async-done(((bf16[16384,256]{1,0:T(8,128)(2,1)}), bf16[512,256]{1,0:T(8,128)(2,1)}) %reduce-scatter.5.cloned.1.call-update) | async-done | bytes 262160 | tf_op jit(solution)/shard_map/reduce_scatter | solution.py:121
  666.6 1.8 bitcast_add_fusion
  (35 shorter events, 0.4 us)
Async XLA Ops:
  7.2 98.3 %copy-start = (bf16[1,32,1,128,128]{4,3,2,1,0:T(8,128)(2,1)S(1)}, bf16[1,32,1,128,128]{4,3,2,1,0:T(8,128)(2,1)}, u32[]{:S(2)}) copy-start(bf16[1,32,1,128,128]{4,3,2,1,0:T(8,128)(2,1)} %param.17) | copy-start | bytes 3145732
  7.2 3.5 copy-start.2
  7.2 77.8 %all-gather.3.cloned.1.call-start = ((), (), s32[]{:S(2)}) async-start(), calls=%async_computation.2 | async-start | bytes 8650752 | tf_op jit(solution)/shard_map/all_gather | solution.py:71
  9.2 204.3 %reduce-scatter.3.cloned.1.call-start = ((), (), s32[]{:S(2)}) async-start(), calls=%async_computation.3 | async-start | bytes 4718592 | tf_op jit(solution)/shard_map/reduce_scatter | solution.py:85
  12.6 2.3 copy-start.11
  12.6 2.5 copy-start.8
  108.1 5.5 copy-start.6
  123.7 89.7 %copy-start.5 = (bf16[256,256]{1,0:T(8,128)(2,1)S(1)}, bf16[256,256]{1,0:T(8,128)(2,1)}, u32[]{:S(2)}) copy-start(bf16[256,256]{1,0:T(8,128)(2,1)} %param.11) | copy-start | bytes 393220
  123.7 89.7 %copy-start.9 = (bf16[512,256]{1,0:T(8,128)(2,1)S(1)}, bf16[512,256]{1,0:T(8,128)(2,1)}, u32[]{:S(2)}) copy-start(bf16[512,256]{1,0:T(8,128)(2,1)} %param.13) | copy-start | bytes 786436
  123.7 89.7 %copy-start.10 = (f32[256]{0:T(256)S(1)}, f32[256]{0:T(256)}, u32[]{:S(2)}) copy-start(f32[256]{0:T(256)} %param.12) | copy-start | bytes 3076
  123.7 152.1 %all-gather.5.cloned.1.call-start = ((), (), s32[]{:S(2)}) async-start(), calls=%async_computation.4 | async-start | bytes 2359296 | tf_op jit(solution)/shard_map/all_gather | solution.py:97
  213.4 3.5 copy-start.4
  216.7 318.5 %all-reduce.2.cloned.1.call-start = ((), (), s32[]{:S(2)}) async-start(), calls=%async_computation.6 | async-start | bytes 524288 | tf_op jit(solution)/shard_map/psum | solution.py:99
  217.9 448.7 %reduce-scatter.5.cloned.1.call-start = ((), (), s32[]{:S(2)}) async-start(), calls=%async_computation.5 | async-start | bytes 8650752 | tf_op jit(solution)/shard_map/reduce_scatter | solution.py:121
  296.8 240.1 %copy-start.1 = (bf16[4096,256]{1,0:T(8,128)(2,1)S(1)}, bf16[4096,256]{1,0:T(8,128)(2,1)}, u32[]{:S(2)}) copy-start(bf16[4096,256]{1,0:T(8,128)(2,1)} %all-gather.5.cloned.1.call-done) | copy-start | bytes 6291460
  535.2 3.0 copy-start.3
  538.7 2.0 copy-start.7
Sparse Core Ops, SparseCore 0:
  10.4 74.5 all-gather.2
  123.9 89.5 reduce-scatter.2
  216.8 59.0 all-gather.4
  281.7 253.4 all-reduce.1
  537.6 128.9 reduce-scatter.4
where the time goes:
time: 676 us; the launch traced here: 675 us
  waiting for transfers between devices  576 us (85%)
  matrix products  42.2 us (6%)
  local copies, waits for them, and re-layouts  28.6 us (4%)
  other arithmetic  14.4 us (2%)
  between operations  13.9 us (2%)
    psum x1, waiting for transfers between devices, on_device(): lax.psum(weight_term, ('dom', 'repl')) * (1.0 / math.sqrt(node_total))  238 us
    reduce_scatter x1, waiting for transfers between devices, on_device(): lax.psum_scatter(placed.reshape(row_count, feat_width).astype(jnp.bfloat1...  123 us
    reduce_scatter x1, waiting for transfers between devices, on_device(): lax.psum_scatter(group_partial, 'repl', scatter_dimension=0, tiled=True)  89.6 us
    all_gather x1, waiting for transfers between devices, on_device(): shard_rows = lax.all_gather(reduced, 'dom', axis=0, tiled=True)  66.3 us
    all_gather x1, waiting for transfers between devices, on_device(): group_grad = lax.all_gather(grad_rows, 'repl', axis=0, tiled=True)  57.9 us
    dot_general x4, matrix products, select(): jnp.einsum(form, hot, values, preferred_element_type=jnp.float32)  17.5 us
    dot_general x4, local copies, waits for them, and re-layouts, tile_product(): return jnp.einsum(form, tiles, values, preferred_element_type=jnp.float32)  15.4 us
  transfers between devices with their start and end apart: 5, of which 5 were waited for; matrix products, arithmetic and copies ran while one was open for 6% of the time, Pallas kernels for 0%

commit v1 on v0

--- a/solution.py
+++ b/solution.py
@@ -68,7 +68,9 @@
     partial_sum = precise_total_sum(
         "qr,qaf->raf", membership_flags(near_row_ids, blocks_dom, jnp.float32), near_prod
     )
-    shard_rows = lax.all_gather(reduced, "dom", axis=0, tiled=True)
+    shard_rows = jnp.concatenate(
+        lax.all_to_all(jnp.stack([reduced] * lax.axis_size("dom")), "dom", 0, 0), axis=0
+    )
     range_count = shard_rows.shape[0] // rows_dev
     tiles = far_block
     row_ids = far_row_ids

time: 676 us -> 801 us (1.18)
  waiting for transfers between devices: 576 us -> 689 us
  starting transfers between devices: 0.39 us -> 10.5 us
    all_to_all x0 -> x1, waiting for transfers between devices: none -> 178 us  [on_device(): lax.all_to_all(jnp.stack([reduced] * lax.axis_size('dom')), 'dom', 0, 0)]
    all_gather x1 -> x0, waiting for transfers between devices: 66.3 us -> none  [on_device(): shard_rows = lax.all_gather(reduced, 'dom', axis=0, tiled=True)]
    all_to_all x0 -> x1, starting transfers between devices: none -> 10.1 us  [on_device(): lax.all_to_all(jnp.stack([reduced] * lax.axis_size('dom')), 'dom', 0, 0)]
  transfers between devices with their start and end apart: 5 -> 5, of which waited for: 5 -> 5; matrix products, arithmetic and copies ran while one was open for 6% -> 5% of each run, Pallas kernels for 0% -> 0%
where the time goes in v1:
time: 801 us
  waiting for transfers between devices  689 us (86%)
  matrix products  41.2 us (5%)
  local copies, waits for them, and re-layouts  32.8 us (4%)
  between operations  13.9 us (2%)
  other arithmetic  13.6 us (2%)
  starting transfers between devices  10.5 us (1%)
    psum x1, waiting for transfers between devices, on_device(): lax.psum(weight_term, ('dom', 'repl')) * (1.0 / math.sqrt(node_total))  239 us
    all_to_all x1, waiting for transfers between devices, on_device(): lax.all_to_all(jnp.stack([reduced] * lax.axis_size('dom')), 'dom', 0, 0)  178 us
    reduce_scatter x1, waiting for transfers between devices, on_device(): lax.psum_scatter(placed.reshape(row_count, feat_width).astype(jnp.bfloat1...  123 us
    reduce_scatter x1, waiting for transfers between devices, on_device(): lax.psum_scatter(group_partial, 'repl', scatter_dimension=0, tiled=True)  91.2 us
    all_gather x1, waiting for transfers between devices, on_device(): group_grad = lax.all_gather(grad_rows, 'repl', axis=0, tiled=True)  57.9 us
    dot_general x4, matrix products, select(): jnp.einsum(form, hot, values, preferred_element_type=jnp.float32)  16.5 us
  transfers between devices with their start and end apart: 5, of which 5 were waited for; matrix products, arithmetic and copies ran while one was open for 5% of the time, Pallas kernels for 0%

profile of v1, /device:TPU:2, one launch (start us, length us, event | category | flops | bytes accessed | tf_op | source)
XLA Modules:
  0.0 800.5 jit_solution(6775724517601051763)
XLA Ops:
  7.2 1.2 convert_element_type.53
  8.3 4.2 stack.2
  12.5 10.1 %all-to-all-start = ((bf16[32,512,256]{2,1,0:T(8,128)(2,1)}), bf16[32,512,256]{2,1,0:T(8,128)(2,1)}, u32[]{:S(2)}, u32[]{:S(2)}) async-start(bf16[32,512,256]{2,1,0:T(8,128)(2,1)} %stack.2), calls=%async_computation | async-start | bytes 16777216 | tf_op jit(solution)/shard_map/all_to_all | solution.py:72
  22.7 0.5 convolution_convert_fusion.1
  23.3 1.9 convolution_bitcast_fusion.3
  25.1 2.3 copy.19
  27.7 3.6 fusion.28
  31.3 177.5 %all-to-all-done = bf16[32,512,256]{2,1,0:T(8,128)(2,1)} async-done(((bf16[32,512,256]{2,1,0:T(8,128)(2,1)}), bf16[32,512,256]{2,1,0:T(8,128)(2,1)}, u32[]{:S(2)}, u32[]{:S(2)}) %all-to-all-start) | async-done | bytes 8388640 | tf_op jit(solution)/shard_map/all_to_all | solution.py:72
  208.8 11.8 %fusion = bf16[32,1,128,256]{3,1,2,0:T(2,128)(2,1)} fusion(bf16[32,4,128,256]{3,2,1,0:T(8,128)(2,1)} %bitcast.10, pred[32,4,1,1]{1,0,2,3:T(32,128)(4,1)S(1)} %get-tuple-element.6), kind=kOutput, calls=%fused_computation.1 | convolution fusion | flops 8388608 | bytes 10485888 | tf_op jit(solution)/shard_map/kqc,kcbf->kqbf/dot_general | solution.py:22
  220.6 8.6 %copy.31 = bf16[32,1,128,256]{2,3,0,1:T(8,128)(2,1)S(1)} copy(bf16[32,1,128,256]{3,1,2,0:T(2,128)(2,1)} %fusion) | data formatting | bytes 4194304 | tf_op jit(solution)/shard_map/kqc,kcbf->kqbf/dot_general | solution.py:22
  229.2 2.7 convolution_bitcast_fusion.1
  231.9 5.5 copy.20
  237.4 5.7 convolution_add_fusion
  243.1 4.4 copy.21
  247.6 91.2 %reduce-scatter.3.cloned.1.call-done = f32[512,256]{1,0:T(8,128)} async-done(((f32[4096,256]{1,0:T(8,128)}), f32[512,256]{1,0:T(8,128)}) %reduce-scatter.3.cloned.1.call-update) | async-done | bytes 524304 | tf_op jit(solution)/shard_map/reduce_scatter | solution.py:87
  338.9 2.2 multiply_convert_fusion.1
  341.1 1.0 convolution_convert_fusion.2
  342.1 1.0 fusion.14
  343.1 0.2 reduce-scatter.5.cloned.1.call-start
  343.4 57.9 %all-gather.2.cloned.1.call-done = bf16[4096,256]{1,0:T(8,128)(2,1)} async-done(((bf16[512,256]{1,0:T(8,128)(2,1)}), bf16[4096,256]{1,0:T(8,128)(2,1)}) %all-gather.2.cloned.1.call-update) | async-done | bytes 2097168 | tf_op jit(solution)/shard_map/all_gather | solution.py:99
  401.3 2.9 convolution_convert_fusion
  404.2 3.7 convolution_bitcast_fusion
  407.9 5.6 copy.24
  413.5 8.7 %multiply_convert_fusion = bf16[32,4,128,256]{3,2,1,0:T(8,128)(2,1)} fusion(f32[32,128,256]{2,1,0:T(8,128)} %copy.24, f32[32,4]{1,0:T(8,128)S(1)} %get-tuple-element.5), kind=kLoop, calls=%fused_computation | loop fusion | flops 8388608 | bytes 12583424 | tf_op jit(solution)/shard_map/convert_element_type | solution.py:124
  422.3 238.5 %all-reduce.2.cloned.1.call-done = f32[256,256]{1,0:T(8,128)} async-done(((f32[256,256]{1,0:T(8,128)}), f32[256,256]{1,0:T(8,128)}) %all-reduce.2.cloned.1.call-update) | async-done | bytes 262160 | tf_op jit(solution)/shard_map/psum | solution.py:101
  660.8 1.7 broadcast_multiply_fusion
  662.5 1.2 fusion.6
  663.8 0.5 convolution_bitcast_fusion.2
  664.3 2.0 copy.27
  666.3 2.4 fusion.33
  668.8 123.3 %reduce-scatter.5.cloned.1.call-done = bf16[512,256]{1,0:T(8,128)(2,1)} async-done(((bf16[16384,256]{1,0:T(8,128)(2,1)}), bf16[512,256]{1,0:T(8,128)(2,1)}) %reduce-scatter.5.cloned.1.call-update) | async-done | bytes 262160 | tf_op jit(solution)/shard_map/reduce_scatter | solution.py:123
  792.2 1.8 bitcast_add_fusion
  (35 shorter events, 0.6 us)
Async XLA Ops:
  7.2 222.0 %copy-start = (bf16[1,32,1,128,128]{4,3,2,1,0:T(8,128)(2,1)S(1)}, bf16[1,32,1,128,128]{4,3,2,1,0:T(8,128)(2,1)}, u32[]{:S(2)}) copy-start(bf16[1,32,1,128,128]{4,3,2,1,0:T(8,128)(2,1)} %param.17) | copy-start | bytes 3145732
  12.5 10.2 %copy-start.7 = (s32[1,16]{1,0:T(1,128)S(1)}, s32[1,16]{1,0:T(1,128)}, u32[]{:S(2)}) copy-start(s32[1,16]{1,0:T(1,128)} %param.16) | copy-start | bytes 196
  12.5 10.7 %copy-start.2 = (bf16[16,128,128]{2,1,0:T(8,128)(2,1)S(1)}, bf16[16,128,128]{2,1,0:T(8,128)(2,1)}, u32[]{:S(2)}) copy-start(bf16[16,128,128]{2,1,0:T(8,128)(2,1)} %param.14) | copy-start | bytes 1572868
  12.5 196.3 %all-to-all-start = ((bf16[32,512,256]{2,1,0:T(8,128)(2,1)}), bf16[32,512,256]{2,1,0:T(8,128)(2,1)}, u32[]{:S(2)}, u32[]{:S(2)}) async-start(bf16[32,512,256]{2,1,0:T(8,128)(2,1)} %stack.2), calls=%async_computation | async-start | bytes 16777216 | tf_op jit(solution)/shard_map/all_to_all | solution.py:72
  22.7 316.2 %reduce-scatter.3.cloned.1.call-start = ((), (), s32[]{:S(2)}) async-start(), calls=%async_computation.3 | async-start | bytes 4718592 | tf_op jit(solution)/shard_map/reduce_scatter | solution.py:87
  25.1 2.3 copy-start.11
  25.1 2.5 copy-start.8
  231.9 5.5 copy-start.6
  247.5 91.3 %copy-start.5 = (bf16[256,256]{1,0:T(8,128)(2,1)S(1)}, bf16[256,256]{1,0:T(8,128)(2,1)}, u32[]{:S(2)}) copy-start(bf16[256,256]{1,0:T(8,128)(2,1)} %param.11) | copy-start | bytes 393220
  247.5 91.3 %copy-start.9 = (bf16[512,256]{1,0:T(8,128)(2,1)S(1)}, bf16[512,256]{1,0:T(8,128)(2,1)}, u32[]{:S(2)}) copy-start(bf16[512,256]{1,0:T(8,128)(2,1)} %param.13) | copy-start | bytes 786436
  247.5 91.3 %copy-start.10 = (f32[256]{0:T(256)S(1)}, f32[256]{0:T(256)}, u32[]{:S(2)}) copy-start(f32[256]{0:T(256)} %param.12) | copy-start | bytes 3076
  247.6 153.7 %all-gather.2.cloned.1.call-start = ((), (), s32[]{:S(2)}) async-start(), calls=%async_computation.4 | async-start | bytes 2359296 | tf_op jit(solution)/shard_map/all_gather | solution.py:99
  338.9 3.3 copy-start.4
  342.1 318.7 %all-reduce.2.cloned.1.call-start = ((), (), s32[]{:S(2)}) async-start(), calls=%async_computation.6 | async-start | bytes 524288 | tf_op jit(solution)/shard_map/psum | solution.py:101
  343.1 449.0 %reduce-scatter.5.cloned.1.call-start = ((), (), s32[]{:S(2)}) async-start(), calls=%async_computation.5 | async-start | bytes 8650752 | tf_op jit(solution)/shard_map/reduce_scatter | solution.py:123
  422.2 240.3 %copy-start.1 = (bf16[4096,256]{1,0:T(8,128)(2,1)S(1)}, bf16[4096,256]{1,0:T(8,128)(2,1)}, u32[]{:S(2)}) copy-start(bf16[4096,256]{1,0:T(8,128)(2,1)} %all-gather.2.cloned.1.call-done) | copy-start | bytes 6291460
  660.8 3.0 copy-start.3
Sparse Core Ops, SparseCore 0:
  247.7 91.1 reduce-scatter.2
  342.2 59.0 all-gather.1
  407.3 253.4 all-reduce.1
  663.2 128.9 reduce-scatter.4
